TPU v7x, 32 devices: a whole 2x2x4 slice. The times are simulated.
32 devices in a mesh: row: 4 (over x, core), col: 8 (over z, y).
Axes of the slice: x: 2, y: 2, z: 4, core: 2. Of those that a mesh axis runs over, the one named last changes fastest.
Arguments:
- p_valence: bfloat16 [4096, 4096], P('row', 'col'), as said below
- p_conduction: bfloat16 [4096, 4096], P('row', 'col'), as said below
- trial_vectors: bfloat16 [2, 4096, 4096], P(None, 'row', 'col'), may hold values from -6 to 6
- mask_valence: int32 [32, 32], replicated, may hold values from 0 to 1, as said below
- mask_conduction: int32 [32, 32], replicated, may hold values from 0 to 1, as said below
- mask_trial: int32 [32, 32], replicated, may hold values 0 or 1
- orbitals: bfloat16 [32, 128, 8192], P('row'), may hold values from -0.29882812 to 0.29882812
- sphere_starts: int32 [32], replicated, may hold values from 0 to 16, as said below
Outputs:
- kernel: bfloat16 [2, 4096, 4096], P(None, 'row', 'col')
- density: float32 [2, 16384], P(None, ('row', 'col'))
Inputs may be any that keep to these rules, and one draw needn't show every extreme that they name: `mask_valence`: symmetric, ones on the block diagonal and next to it. `mask_conduction`: symmetric, ones on the block diagonal and next to it. `p_valence`: symmetric. `p_conduction`: symmetric. `sphere_starts`: the first block's start is 0 and the last block's 32 - 16.
All inputs are finite; a program needn't handle non-finite values.
Results may differ from a plain program's by a relative error of at most 0.0049.
Values may be sent and summed in bfloat16 or wider, within the bound.
A program may use at most 320 MiB of HBM per device.

v0:
```python
import jax
import jax.numpy as jnp
from jax import lax
from jax.sharding import PartitionSpec as P

BS = 128
SPAN = 16
SP = 512


def broadcast(x, axis, root):
    mine = lax.axis_index(axis) == root
    return lax.psum(jnp.where(mine, x, jnp.zeros_like(x)), axis)


def masked(values, block_mask, row_index, col_index):
    leading_dims = values.shape[:-2]
    row_blocks = values.shape[-2] // BS
    col_blocks = values.shape[-1] // BS
    tile_mask = lax.dynamic_slice(
        block_mask, (row_index * row_blocks, col_index * col_blocks), (row_blocks, col_blocks)
    ).astype(values.dtype)
    shaped = values.reshape(leading_dims + (row_blocks, BS, col_blocks, BS))
    return (shaped * tile_mask[:, None, :, None]).reshape(values.shape)


def local(
    p_valence,
    p_conduction,
    trial_vectors,
    mask_valence,
    mask_conduction,
    mask_trial,
    orbitals,
    sphere_starts,
):
    row_index = lax.axis_index("row")
    col_index = lax.axis_index("col")
    valence = masked(p_valence, mask_valence, row_index, col_index)
    conduction = masked(p_conduction, mask_conduction, row_index, col_index)
    trials = masked(trial_vectors, mask_trial, row_index, col_index)
    vector_count = trials.shape[0]
    local_rows = trials.shape[1]
    local_cols = trials.shape[2]
    panels = lax.all_gather(trials, "col", axis=2, tiled=True)
    response = jnp.einsum(
        "vik,kj->vij",
        panels,
        lax.all_gather(conduction, "row", axis=0, tiled=True),
        preferred_element_type=jnp.float32,
    )
    response_half = response.astype(jnp.bfloat16)
    gathered = lax.all_gather(response_half, "row", axis=1, tiled=True)
    kernel_sum = jnp.einsum(
        "ik,vkj->vij",
        lax.all_gather(valence, "col", axis=1, tiled=True),
        gathered,
        preferred_element_type=jnp.float32,
    )
    kernel = masked(kernel_sum, mask_trial, row_index, col_index).astype(jnp.bfloat16)
    row_blocks = local_rows // BS
    col_blocks = local_cols // BS
    ratio = lax.axis_size("col") // lax.axis_size("row")
    own_part = lax.dynamic_slice_in_dim(orbitals, col_index % ratio * col_blocks, col_blocks, 0)
    partner = broadcast(own_part, "row", col_index // ratio)
    partner_padded = jnp.pad(
        partner.reshape(col_blocks, BS, SPAN, SP), ((0, 0), (0, 0), (SPAN, SPAN), (0, 0))
    )
    starts_rows = lax.dynamic_slice_in_dim(sphere_starts, row_index * row_blocks, row_blocks, 0)
    starts_cols = lax.dynamic_slice_in_dim(sphere_starts, col_index * col_blocks, col_blocks, 0)
    offsets = jnp.clip(starts_rows[:, None] - starts_cols[None, :] + SPAN, 0, 2 * SPAN)

    def take_frame(orbital_block, offset):
        return lax.dynamic_slice_in_dim(orbital_block, offset, SPAN, 1)

    def frames_for_row(offset_row):
        return jax.vmap(take_frame)(partner_padded, offset_row)

    frames = jax.vmap(frames_for_row)(offsets).reshape(row_blocks, col_blocks, BS, SPAN * SP)
    kernel_blocks = kernel.reshape(vector_count, row_blocks, BS, col_blocks, BS).transpose(
        0, 1, 3, 2, 4
    )
    applied = jnp.einsum(
        "vabmn,abnp->vamp", kernel_blocks, frames, preferred_element_type=jnp.float32
    )
    contrib = jnp.sum(orbitals[None] * applied, axis=2)
    slab_count = lax.axis_size("row") * lax.axis_size("col")
    density_grid = jnp.zeros((vector_count, slab_count, SP), jnp.float32)
    zero_index = jnp.zeros((), jnp.int32)
    for local_block in range(row_blocks):
        begin_slab = starts_rows[local_block]
        current = lax.dynamic_slice(
            density_grid, (zero_index, begin_slab, zero_index), (vector_count, SPAN, SP)
        )
        update = current + contrib[:, local_block].reshape(vector_count, SPAN, SP)
        density_grid = lax.dynamic_update_slice(
            density_grid, update, (zero_index, begin_slab, zero_index)
        )
    own_slab = lax.psum_scatter(density_grid, ("row", "col"), scatter_dimension=1, tiled=True)
    density = own_slab.reshape(vector_count, SP)
    return (kernel, density)


def solution(mesh):
    placed = (
        P("row", "col"),
        P("row", "col"),
        P(None, "row", "col"),
        P(),
        P(),
        P(),
        P("row", None, None),
        P(),
    )
    return jax.shard_map(
        local,
        mesh=mesh,
        in_specs=placed,
        out_specs=(P(None, "row", "col"), P(None, ("row", "col"))),
        check_vma=False,
    )
```

profile of v0, /device:TPU:0, one launch (start us, length us, event | category | flops | bytes accessed | tf_op | source)
XLA Modules:
  0.0 935.6 jit_solution(7683359424325019603)
XLA Ops:
  13.9 7.4 dynamic-slice_select_fusion
  21.2 11.8 %copy.28 = bf16[64,8,16,512]{3,2,1,0:T(8,128)(2,1)} copy(bf16[64,8,16,512]{3,1,2,0:T(8,128)(2,1)} %bitcast.123) | data formatting | bytes 16777216
  35.6 18.6 %convert_element_type.30 = f32[8,128,8192]{2,1,0:T(8,128)} convert(bf16[8,128,8192]{2,1,0:T(8,128)(2,1)} %param.14) | non-fusion elementwise | flops 8388608 | bytes 50331648 | tf_op jit(solution)/shard_map/convert_element_type | solution.py:86
  65.0 213.2 %all-gather.5.cloned.1.call-done = bf16[2,1024,4096]{2,1,0:T(8,128)(2,1)} async-done(((bf16[2,1024,512]{2,1,0:T(8,128)(2,1)}), bf16[2,1024,4096]{2,1,0:T(8,128)(2,1)}) %all-gather.5.cloned.1.call-update) | async-done | bytes 16777232 | tf_op jit(solution)/shard_map/all_gather | solution.py:45
  278.2 14.5 %fusion.13 = bf16[2,1024,512]{2,1,0:T(8,128)(2,1)} fusion(bf16[2,1024,4096]{2,1,0:T(8,128)(2,1)} %all-gather.5.cloned.1.call-done, bf16[4096,512]{1,0:T(8,128)(2,1)} %all-gather.7.cloned.1.call-done), kind=kOutput, calls=%fused_computation.15 | convolution fusion | flops 8590983168 | bytes 23068672 | tf_op jit(solution)/shard_map/vik,kj->vij/dot_general | solution.py:46
  298.9 132.9 %all-reduce.5.cloned.1.call-done = bf16[4,128,16,512]{3,2,1,0:T(8,128)(2,1)} async-done(((bf16[4,128,16,512]{3,2,1,0:T(8,128)(2,1)}), bf16[4,128,16,512]{3,2,1,0:T(8,128)(2,1)}) %all-reduce.5.cloned.1.call-update) | async-done | bytes 8388624 | tf_op jit(solution)/shard_map/psum | solution.py:13
  431.8 12.1 %pad.4 = bf16[4,128,48,512]{3,2,1,0:T(8,128)(2,1)} pad(bf16[4,128,16,512]{3,2,1,0:T(8,128)(2,1)} %all-reduce.5.cloned.1.call-done, bf16[]{:T(256)} %constant.48.clone.1), padding=0_0x0_0x16_16x0_0 | pad | bytes 33554432 | tf_op jit(solution)/shard_map/jit(_pad)/pad | solution.py:66
  443.9 204.5 %while.1 = (s32[]{:T(128)}, bf16[4,128,48,512]{3,2,1,0:T(8,128)(2,1)}, s32[32,4]{0,1:T(4,128)S(1)}, bf16[32,128,16,512]{3,2,1,0:T(8,128)(2,1)}, s32[]{:T(128)}) while((s32[]{:T(128)}, bf16[4,128,48,512]{3,2,1,0:T(8,128)(2,1)}, s32[32,4]{0,1:T(4,128)S(1)}, bf16[32,128,16,512]{3,2,1,0:T(8,128)(2,1)}, s32[]{:T(128)}) %tuple.42), condition=%wide.while_cond, body=%wide.while_body.sunk | while | flops 2 | bytes 4195953 | solution.py:74
  444.6 5.7 dynamic-slice_dynamic-update-slice_fusion.2
  457.3 5.8 dynamic-slice_dynamic-update-slice_fusion.2
  463.7 5.7 dynamic-slice_dynamic-update-slice_fusion.2
  470.1 5.7 dynamic-slice_dynamic-update-slice_fusion.2
  482.9 5.7 dynamic-slice_dynamic-update-slice_fusion.2
  489.3 5.7 dynamic-slice_dynamic-update-slice_fusion.2
  502.1 5.7 dynamic-slice_dynamic-update-slice_fusion.2
  508.4 5.7 dynamic-slice_dynamic-update-slice_fusion.2
  514.8 5.7 dynamic-slice_dynamic-update-slice_fusion.2
  521.2 5.7 dynamic-slice_dynamic-update-slice_fusion.2
  534.0 5.8 dynamic-slice_dynamic-update-slice_fusion.2
  553.1 5.7 dynamic-slice_dynamic-update-slice_fusion.2
  565.8 6.2 dynamic-slice_dynamic-update-slice_fusion.2
  572.7 5.7 dynamic-slice_dynamic-update-slice_fusion.2
  585.4 5.7 dynamic-slice_dynamic-update-slice_fusion.2
  591.7 5.8 dynamic-slice_dynamic-update-slice_fusion.2
  598.2 5.7 dynamic-slice_dynamic-update-slice_fusion.2
  604.6 5.7 dynamic-slice_dynamic-update-slice_fusion.2
  617.3 5.7 dynamic-slice_dynamic-update-slice_fusion.2
  623.7 5.7 dynamic-slice_dynamic-update-slice_fusion.2
  648.4 98.3 %reshape.126 = bf16[8,4,128,8192,1]{3,2,1,0,4:T(8,128)(2,1)} reshape(bf16[32,128,16,512]{3,2,1,0:T(8,128)(2,1)} %get-tuple-element.9) | data formatting | bytes 134217728 | tf_op jit(solution)/shard_map/reshape | solution.py:79
  746.8 13.8 %fusion.7 = bf16[2,1024,512]{1,2,0:T(8,128)(2,1)S(1)} fusion(bf16[2,4096,512]{2,1,0:T(8,128)(2,1)} %all-gather.9.cloned.1.call-done, bf16[1024,4096]{1,0:T(8,128)(2,1)} %all-gather.11.cloned.1.call-done, f32[1024,512]{0,1:T(8,128)S(1)} %bitcast.131), kind=kOutput, calls=%fused_computation.10 | convolution fusion | flops 8592031744 | bytes 20971520 | tf_op jit(solution)/shard_map/ik,vkj->vij/dot_general | solution.py:54
  765.7 33.2 %fusion = f32[2,8,8192]{2,0,1:T(2,128)S(1)} fusion(f32[8,128,8192]{2,1,0:T(8,128)} %convert_element_type.30, bf16[8,4,128,8192,1]{3,2,1,0,4:T(8,128)(2,1)} %reshape.126, bf16[2,8,128,4,128]{4,2,3,0,1:T(8,128)(2,1)S(1)} %copy.18), kind=kOutput, calls=%fused_computation.3 | convolution fusion | flops 17213292544 | bytes 103284736 | tf_op jit(solution)/shard_map/vabmn,abnp->vamp/dot_general | solution.py:83
  806.6 120.9 %all-reduce.7.cloned.1.call-done = f32[2,32,512]{2,0,1:T(2,128)} async-done(((f32[2,32,512]{2,0,1:T(2,128)}), f32[2,32,512]{2,0,1:T(2,128)}) %all-reduce.7.cloned.1.call-update) | async-done | bytes 131088
  (143 shorter events, 114.4 us)
Async XLA Ops:
  7.2 5.1 copy-start.1
  7.2 57.8 %all-gather.7.cloned.1.call-start = ((), (), s32[]{:S(2)}) async-start(), calls=%async_computation.1 | async-start | bytes 5242880 | tf_op jit(solution)/shard_map/all_gather | solution.py:49
  10.9 267.3 %all-gather.5.cloned.1.call-start = ((), (), s32[]{:S(2)}) async-start(), calls=%async_computation | async-start | bytes 18874368 | tf_op jit(solution)/shard_map/all_gather | solution.py:45
  13.8 418.0 %all-reduce.5.cloned.1.call-start = ((), (), s32[]{:S(2)}) async-start(), calls=%async_computation.4 | async-start | bytes 16777216 | tf_op jit(solution)/shard_map/psum | solution.py:13
  33.0 1.2 copy-start.2
  33.0 2.5 copy-start.3
  33.0 713.7 %all-gather.11.cloned.1.call-start = ((), (), s32[]{:S(2)}) async-start(), calls=%async_computation.3 | async-start | bytes 9437184 | tf_op jit(solution)/shard_map/all_gather | solution.py:56
  35.4 711.3 %all-gather.9.cloned.1.call-start = ((), (), s32[]{:S(2)}) async-start(), calls=%async_computation.2 | async-start | bytes 10485760 | tf_op jit(solution)/shard_map/all_gather | solution.py:53
  292.8 634.7 %all-reduce.7.cloned.1.call-start = ((), (), s32[]{:S(2)}) async-start(), calls=%async_computation.5 | async-start | bytes 262144
  760.5 2.0 copy-start
Sparse Core Ops, SparseCore 0:
  11.0 37.2 all-gather.6
  50.9 227.2 all-gather.4
  280.7 151.0 all-reduce.4
  433.7 125.0 all-gather.10
  560.8 56.4 all-gather.8
  802.8 124.6 all-reduce.6
where the time goes:
time: 941 us; the launch traced here: 936 us
  waiting for transfers between devices  467 us (50%)
  local copies, waits for them, and re-layouts  344 us (37%)
  matrix products  61.5 us (7%)
  other arithmetic  32.9 us (3%)
  between operations  29.5 us (3%)
    all_gather x1, waiting for transfers between devices, local(): panels = lax.all_gather(trials, 'col', axis=2, tiled=True)  213 us
    gather x96, local copies, waits for them, and re-layouts  204 us
    psum x1, waiting for transfers between devices, broadcast(): return lax.psum(jnp.where(mine, x, jnp.zeros_like(x)), axis)  133 us
    unnamed x7, waiting for transfers between devices  121 us
    reshape x1, local copies, waits for them, and re-layouts, local(): jax.vmap(frames_for_row)(offsets)  98.3 us
    dot_general x1, matrix products, local(): jnp.einsum('vabmn,abnp->vamp', kernel_blocks, frames, preferred_element_t...  33.2 us
    unnamed x15, local copies, waits for them, and re-layouts  19.2 us
  transfers between devices with their start and end apart: 6, of which 3 were waited for; matrix products, arithmetic and copies ran while one was open for 40% of the time, Pallas kernels for 0%

commit v1 on v0

--- a/solution.py
+++ b/solution.py
@@ -42,7 +42,8 @@
     vector_count = trials.shape[0]
     local_rows = trials.shape[1]
     local_cols = trials.shape[2]
-    panels = lax.all_gather(trials, "col", axis=2, tiled=True)
+    pieces = lax.all_gather(trials, "col", axis=0, tiled=False)
+    panels = jnp.concatenate(pieces, axis=2)
     response = jnp.einsum(
         "vik,kj->vij",
         panels,

time: 941 us -> 941 us (level)
  waiting for transfers between devices: 467 us -> 444 us
  local copies, waits for them, and re-layouts: 344 us -> 366 us
    all_gather x1, waiting for transfers between devices: 213 us -> 176 us  [local(): pieces = lax.all_gather(trials, 'col', axis=0, tiled=False)]
    reshape x0 -> x1, local copies, waits for them, and re-layouts: none -> 21.9 us  [local(): panels = jnp.concatenate(pieces, axis=2)]
    all_gather x1, waiting for transfers between devices: 0.01 us -> 12.4 us  [local(): lax.all_gather(conduction, 'row', axis=0, tiled=True)]
  transfers between devices with their start and end apart: 6 -> 6, of which waited for: 3 -> 4; matrix products, arithmetic and copies ran while one was open for 40% -> 43% of each run, Pallas kernels for 0% -> 0%
where the time goes in v1:
time: 941 us; the launch traced here: 935 us
  waiting for transfers between devices  444 us (47%)
  local copies, waits for them, and re-layouts  366 us (39%)
  matrix products  61.6 us (7%)
  other arithmetic  33.1 us (4%)
  between operations  29.4 us (3%)
    gather x96, local copies, waits for them, and re-layouts  204 us
    all_gather x1, waiting for transfers between devices, local(): pieces = lax.all_gather(trials, 'col', axis=0, tiled=False)  176 us
    psum x1, waiting for transfers between devices, broadcast(): return lax.psum(jnp.where(mine, x, jnp.zeros_like(x)), axis)  135 us
    unnamed x7, waiting for transfers between devices  121 us
    reshape x1, local copies, waits for them, and re-layouts, local(): jax.vmap(frames_for_row)(offsets)  98.3 us
    dot_general x1, matrix products, local(): jnp.einsum('vabmn,abnp->vamp', kernel_blocks, frames, preferred_element_t...  33.2 us
    reshape x1, local copies, waits for them, and re-layouts, local(): panels = jnp.concatenate(pieces, axis=2)  21.9 us
    unnamed x15, local copies, waits for them, and re-layouts  19.7 us
  transfers between devices with their start and end apart: 6, of which 4 were waited for; matrix products, arithmetic and copies ran while one was open for 43% of the time, Pallas kernels for 0%

profile of v1, /device:TPU:0, one launch (start us, length us, event | category | flops | bytes accessed | tf_op | source)
XLA Modules:
  0.0 935.4 jit_solution(14159790307048464209)
XLA Ops:
  14.2 7.2 dynamic-slice_select_fusion
  21.4 12.2 %copy.37 = bf16[64,8,16,512]{3,2,1,0:T(8,128)(2,1)} copy(bf16[64,8,16,512]{3,1,2,0:T(8,128)(2,1)} %bitcast.127) | data formatting | bytes 16777216
  36.2 18.6 %convert_element_type.30 = f32[8,128,8192]{2,1,0:T(8,128)} convert(bf16[8,128,8192]{2,1,0:T(8,128)(2,1)} %param.14) | non-fusion elementwise | flops 8388608 | bytes 50331648 | tf_op jit(solution)/shard_map/convert_element_type | solution.py:87
  65.6 176.3 %all-gather.12.cloned.1.call-done = bf16[16,1024,512]{2,1,0:T(8,128)(2,1)} async-done(((bf16[2,1024,512]{2,1,0:T(8,128)(2,1)}), bf16[16,1024,512]{2,1,0:T(8,128)(2,1)}) %all-gather.12.cloned.1.call-update) | async-done | bytes 16777232 | tf_op jit(solution)/shard_map/all_gather | solution.py:45
  241.9 21.9 %copy.22 = bf16[2,1024,8,512]{1,3,2,0:T(8,128)(2,1)} copy(bf16[2,1024,8,512]{3,1,0,2:T(8,128)(2,1)} %bitcast.128) | data formatting | bytes 33554432 | tf_op jit(solution)/shard_map/reshape | solution.py:46
  263.8 12.4 %all-gather.6.cloned.1.call-done = bf16[4096,512]{1,0:T(8,128)(2,1)} async-done(((bf16[1024,512]{1,0:T(8,128)(2,1)}), bf16[4096,512]{1,0:T(8,128)(2,1)}) %all-gather.6.cloned.1.call-update) | async-done | bytes 4194320 | tf_op jit(solution)/shard_map/all_gather | solution.py:50
  276.1 14.6 %fusion.13 = bf16[2,1024,512]{2,1,0:T(8,128)(2,1)} fusion(bf16[2,1024,4096]{1,2,0:T(8,128)(2,1)} %bitcast.129, bf16[4096,512]{1,0:T(8,128)(2,1)} %all-gather.6.cloned.1.call-done), kind=kOutput, calls=%fused_computation.15 | convolution fusion | flops 8590983168 | bytes 23068672 | tf_op jit(solution)/shard_map/vik,kj->vij/dot_general | solution.py:47
  296.9 134.6 %all-reduce.5.cloned.1.call-done = bf16[4,128,16,512]{3,2,1,0:T(8,128)(2,1)} async-done(((bf16[4,128,16,512]{3,2,1,0:T(8,128)(2,1)}), bf16[4,128,16,512]{3,2,1,0:T(8,128)(2,1)}) %all-reduce.5.cloned.1.call-update) | async-done | bytes 8388624 | tf_op jit(solution)/shard_map/psum | solution.py:13
  431.5 12.1 %pad.4 = bf16[4,128,48,512]{3,2,1,0:T(8,128)(2,1)} pad(bf16[4,128,16,512]{3,2,1,0:T(8,128)(2,1)} %all-reduce.5.cloned.1.call-done, bf16[]{:T(256)} %constant.48.clone.1), padding=0_0x0_0x16_16x0_0 | pad | bytes 33554432 | tf_op jit(solution)/shard_map/jit(_pad)/pad | solution.py:67
  443.7 204.5 %while.1 = (s32[]{:T(128)}, bf16[4,128,48,512]{3,2,1,0:T(8,128)(2,1)}, s32[32,4]{0,1:T(4,128)S(1)}, bf16[32,128,16,512]{3,2,1,0:T(8,128)(2,1)}, s32[]{:T(128)}) while((s32[]{:T(128)}, bf16[4,128,48,512]{3,2,1,0:T(8,128)(2,1)}, s32[32,4]{0,1:T(4,128)S(1)}, bf16[32,128,16,512]{3,2,1,0:T(8,128)(2,1)}, s32[]{:T(128)}) %tuple.43), condition=%wide.while_cond, body=%wide.while_body.sunk | while | flops 2 | bytes 4195953 | solution.py:75
  457.0 5.8 dynamic-slice_dynamic-update-slice_fusion.2
  463.5 5.7 dynamic-slice_dynamic-update-slice_fusion.2
  469.9 5.7 dynamic-slice_dynamic-update-slice_fusion.2
  482.6 5.7 dynamic-slice_dynamic-update-slice_fusion.2
  489.1 5.7 dynamic-slice_dynamic-update-slice_fusion.2
  501.8 5.7 dynamic-slice_dynamic-update-slice_fusion.2
  508.2 5.7 dynamic-slice_dynamic-update-slice_fusion.2
  514.5 5.7 dynamic-slice_dynamic-update-slice_fusion.2
  521.0 5.7 dynamic-slice_dynamic-update-slice_fusion.2
  533.7 5.8 dynamic-slice_dynamic-update-slice_fusion.2
  552.8 5.7 dynamic-slice_dynamic-update-slice_fusion.2
  565.6 6.2 dynamic-slice_dynamic-update-slice_fusion.2
  572.4 5.7 dynamic-slice_dynamic-update-slice_fusion.2
  591.5 5.8 dynamic-slice_dynamic-update-slice_fusion.2
  597.9 5.7 dynamic-slice_dynamic-update-slice_fusion.2
  604.3 5.7 dynamic-slice_dynamic-update-slice_fusion.2
  617.0 5.7 dynamic-slice_dynamic-update-slice_fusion.2
  623.4 5.7 dynamic-slice_dynamic-update-slice_fusion.2
  648.2 98.3 %reshape.136 = bf16[8,4,128,8192,1]{3,2,1,0,4:T(8,128)(2,1)} reshape(bf16[32,128,16,512]{3,2,1,0:T(8,128)(2,1)} %get-tuple-element.9) | data formatting | bytes 134217728 | tf_op jit(solution)/shard_map/reshape | solution.py:80
  746.5 13.8 %fusion.7 = bf16[2,1024,512]{1,2,0:T(8,128)(2,1)S(1)} fusion(bf16[2,4096,512]{2,1,0:T(8,128)(2,1)} %all-gather.8.cloned.1.call-done, bf16[1024,4096]{1,0:T(8,128)(2,1)} %all-gather.10.cloned.1.call-done, f32[1024,512]{0,1:T(8,128)S(1)} %bitcast.137), kind=kOutput, calls=%fused_computation.10 | convolution fusion | flops 8592031744 | bytes 20971520 | tf_op jit(solution)/shard_map/ik,vkj->vij/dot_general | solution.py:55
  765.5 33.2 %fusion = f32[2,8,8192]{2,0,1:T(2,128)S(1)} fusion(f32[8,128,8192]{2,1,0:T(8,128)} %convert_element_type.30, bf16[8,4,128,8192,1]{3,2,1,0,4:T(8,128)(2,1)} %reshape.136, bf16[2,8,128,4,128]{4,2,3,0,1:T(8,128)(2,1)S(1)} %copy.26), kind=kOutput, calls=%fused_computation.3 | convolution fusion | flops 17213292544 | bytes 103284736 | tf_op jit(solution)/shard_map/vabmn,abnp->vamp/dot_general | solution.py:84
  806.4 120.9 %all-reduce.7.cloned.1.call-done = f32[2,32,512]{2,0,1:T(2,128)} async-done(((f32[2,32,512]{2,0,1:T(2,128)}), f32[2,32,512]{2,0,1:T(2,128)}) %all-reduce.7.cloned.1.call-update) | async-done | bytes 131088
  (144 shorter events, 126.1 us)
Async XLA Ops:
  7.2 5.8 copy-start.1
  7.2 234.7 %all-gather.12.cloned.1.call-start = ((), (), s32[]{:S(2)}) async-start(), calls=%async_computation.4 | async-start | bytes 18874368 | tf_op jit(solution)/shard_map/all_gather | solution.py:45
  11.8 264.4 %all-gather.6.cloned.1.call-start = ((), (), s32[]{:S(2)}) async-start(), calls=%async_computation | async-start | bytes 5242880 | tf_op jit(solution)/shard_map/all_gather | solution.py:50
  14.1 417.4 %all-reduce.5.cloned.1.call-start = ((), (), s32[]{:S(2)}) async-start(), calls=%async_computation.3 | async-start | bytes 16777216 | tf_op jit(solution)/shard_map/psum | solution.py:13
  33.6 1.2 copy-start.2
  33.6 2.5 copy-start.3
  33.6 712.9 %all-gather.10.cloned.1.call-start = ((), (), s32[]{:S(2)}) async-start(), calls=%async_computation.2 | async-start | bytes 9437184 | tf_op jit(solution)/shard_map/all_gather | solution.py:57
  36.0 710.5 %all-gather.8.cloned.1.call-start = ((), (), s32[]{:S(2)}) async-start(), calls=%async_computation.1 | async-start | bytes 10485760 | tf_op jit(solution)/shard_map/all_gather | solution.py:54
  290.8 636.5 %all-reduce.7.cloned.1.call-start = ((), (), s32[]{:S(2)}) async-start(), calls=%async_computation.5 | async-start | bytes 262144
  760.3 2.0 copy-start
Sparse Core Ops, SparseCore 0:
  11.9 229.9 all-gather.11
  243.5 32.6 all-gather.5
  278.6 152.8 all-reduce.4
  433.4 125.0 all-gather.9
  560.5 56.4 all-gather.7
  802.5 124.6 all-reduce.6
